TPU v7x, 32 devices: a whole 2x2x4 slice. The times are simulated.
32 devices in a mesh: groups: 1, rank: 32 (over z, y, x, core).
Axes of the slice: x: 2, y: 2, z: 4, core: 2. Of those that a mesh axis runs over, the one named last changes fastest.
Arguments:
- core: float32 [256, 256, 256], P('rank', 'groups'), may hold values from -6 to 6
- x_factor: float32 [1536, 256], P('groups'), may hold values from -0.375 to 0.375
- y_factor: float32 [2048, 256], P('groups'), may hold values from -0.375 to 0.375
- z_factor: float32 [256, 1536], P('rank', 'groups'), may hold values from -0.375 to 0.375
- offsets: int32 [8], P('groups'), may hold values from 0 to 1535, as said below
- initial: float32 [1536, 8, 2048], P('rank', 'groups'), may hold values from -80 to 80
Outputs:
- max_error: float32 [1], P('groups')
- psnr: float32 [8], P('groups')
- ssim_five: float32 [1536, 8, 2048], P('rank', 'groups')
- ssim_seven: float32 [1536, 8, 2048], P('rank', 'groups')
- ssim_eleven: float32 [1536, 8, 2048], P('rank', 'groups')
Inputs may be any that keep to these rules, and one draw needn't show every extreme that they name: `offsets`: 8 distinct planes in increasing order.
All inputs are finite; a program needn't handle non-finite values.
Results may differ from a plain program's by a relative error of at most 0.000075.
Values sent between devices are 32-bit elements; how exact they have to be, the bound alone decides.
A program may use at most 128 MiB of HBM per device.

v0:
```python
import jax
import jax.numpy as jnp
from jax import lax
from jax.sharding import PartitionSpec as P

peak_value = 64.0
first_const = 0.01 * peak_value * (0.01 * peak_value)
second_const = 0.03 * peak_value * (0.03 * peak_value)
epsilon = 1e-06


def padded_2(block, sides, width):
    for axis, dim in sides:
        count = lax.axis_size(axis)
        forward = [(i, i + 1) for i in range(count - 1)]
        backward = [(target, source) for source, target in forward]
        low = lax.ppermute(
            lax.slice_in_dim(block, block.shape[dim] - width, None, axis=dim), axis, forward
        )
        high = lax.ppermute(lax.slice_in_dim(block, 0, width, axis=dim), axis, backward)
        block = jnp.concatenate([low, block, high], axis=dim)
    return block


def similarity(sum_target, sum_rebuilt, sum_tt, sum_rr, sum_tr, window):
    window_area = float(window * window)
    mean_target = sum_target / window_area
    mean_rebuilt = sum_rebuilt / window_area
    var_target = sum_tt / window_area - mean_target * mean_target
    var_rebuilt = sum_rr / window_area - mean_rebuilt * mean_rebuilt
    covar = sum_tr / window_area - mean_target * mean_rebuilt
    upper = (2.0 * mean_target * mean_rebuilt + first_const) * (2.0 * covar + second_const)
    lower = (mean_target * mean_target + mean_rebuilt * mean_rebuilt + first_const) * (
        var_target + var_rebuilt + second_const
    )
    return upper / lower


def window_sums(values, window, length):
    margin = window // 2
    across = values.shape[-1]
    row_sums = values[0:length]
    for step_index in range(1, window):
        row_sums = row_sums + values[step_index : step_index + length]
    padded = jnp.pad(row_sums, ((0, 0), (0, 0), (margin, margin)))
    summed = padded[:, :, 0:across]
    for step_index in range(1, window):
        summed = summed + padded[:, :, step_index : step_index + across]
    return summed


def local_similarity(extended, window, length):
    margin = window // 2
    lowest = 5 - margin
    target_rows = extended[0, lowest : lowest + length + 2 * margin]
    rebuilt_rows = extended[1, lowest : lowest + length + 2 * margin]
    return similarity(
        window_sums(target_rows, window, length),
        window_sums(rebuilt_rows, window, length),
        window_sums(target_rows * target_rows, window, length),
        window_sums(rebuilt_rows * rebuilt_rows, window, length),
        window_sums(target_rows * rebuilt_rows, window, length),
        window,
    )


def body(core, x_factor, y_factor, z_factor, offsets, initial):
    exact = lax.Precision.HIGHEST
    slab = z_factor.shape[0]
    planes = offsets.shape[0]
    across = y_factor.shape[0]
    local_rows = initial.shape[0]
    picked = jnp.take(z_factor, offsets, axis=1)
    contract_form = "kab,kp->bpa"
    split_dim = 2
    all_picked = lax.all_gather(picked, "rank", axis=0, tiled=True)
    regrouped = lax.all_to_all(core, "rank", split_axis=split_dim, concat_axis=0, tiled=True)
    planes_core = jnp.einsum(contract_form, regrouped, all_picked, precision=exact)
    along_x = jnp.einsum("bpa,xa->xbp", planes_core, x_factor, precision=exact).reshape(
        x_factor.shape[0], slab * planes
    )
    rows_block = lax.all_to_all(along_x, "rank", split_axis=0, concat_axis=1, tiled=True).reshape(
        local_rows, -1, planes
    )
    rebuilt = jnp.einsum("xbp,yb->xpy", rows_block, y_factor, precision=exact)
    misfit = initial - rebuilt
    max_error = lax.pmax(jnp.max(jnp.abs(misfit)).reshape(1), "rank")
    square_sums = lax.psum(jnp.sum(misfit * misfit, axis=(0, 2)), "rank")
    mean_square = square_sums / float(x_factor.shape[0] * across)
    psnr = 10.0 * jnp.log10(peak_value * peak_value / (mean_square + epsilon))
    stacked = jnp.stack((initial, rebuilt))
    extended = padded_2(stacked, (("rank", 1),), 5)
    ssim_five = local_similarity(extended, 5, local_rows)
    ssim_seven = local_similarity(extended, 7, local_rows)
    ssim_eleven = local_similarity(extended, 11, local_rows)
    return (max_error, psnr, ssim_five, ssim_seven, ssim_eleven)


def solution(mesh):
    placed = (
        P("rank", "groups", None),
        P("groups", None),
        P("groups", None),
        P("rank", "groups"),
        P("groups"),
        P("rank", "groups", None),
    )
    return jax.shard_map(
        body,
        mesh=mesh,
        in_specs=placed,
        out_specs=(
            P("groups"),
            P("groups"),
            P("rank", "groups", None),
            P("rank", "groups", None),
            P("rank", "groups", None),
        ),
        check_vma=False,
    )
```

profile of v0, /device:TPU:0, one launch (start us, length us, event | category | flops | bytes accessed | tf_op | source)
XLA Modules:
  0.0 499.6 jit_solution(9895086955580270290)
XLA Ops:
  0.7 3.2 copy.19
  3.9 7.5 %all-to-all-start = ((f32[8,256,256]{1,0,2:T(8,128)}), f32[8,256,256]{1,0,2:T(8,128)}, u32[]{:S(2)}, u32[]{:S(2)}) async-start(f32[8,256,256]{1,0,2:T(8,128)} %copy.19), calls=%async_computation | async-start | bytes 4194304 | tf_op jit(solution)/shard_map/all_to_all | solution.py:77
  12.3 69.1 %all_gather.3 = f32[256,8]{1,0:T(8,128)S(1)} all-gather(f32[8,8]{1,0:T(8,128)S(1)} %copy.18), channel_id=1, replica_groups=mesh['groups'=1,'rank'=32] {'rank'}, dimensions={0}, use_global_device_ids=true | all-gather | bytes 8448 | tf_op jit(solution)/shard_map/all_gather | solution.py:76
  91.0 19.7 %all_to_all.34 = f32[32,1,3072]{2,1,0:T(1,128)S(1)} all-to-all(f32[32,1,3072]{2,1,0:T(1,128)S(1)} %reshape.233), channel_id=1, replica_groups=mesh['groups'=1,'rank'=32] {'rank'}, dimensions={0} | all-to-all | bytes 786432 | tf_op jit(solution)/shard_map/all_to_all | solution.py:82
  120.1 3.2 collective-permute-start
  125.6 4.2 slice_multiply_fusion.7
  131.8 4.3 slice_multiply_fusion.4
  136.0 3.8 pad_maximum_fusion.1
  139.8 7.1 %add_add_fusion.3 = (f32[48,8,2048]{2,1,0:T(8,128)}, f32[48,8,2048]{2,1,0:T(8,128)}, f32[]{:T(128)}, f32[8]{0:T(128)S(1)}) fusion(f32[48,8,2048]{2,1,0:T(8,128)} %param.11, f32[2,53,8,2048]{3,2,1,0:T(8,128)S(1)} %get-tuple-element.25, f32[2,53,8,2048]{3,2,1,0:T(8,128)S(1)} %get-tuple-element.24, f32[48,8,2048]{2,1,0:T(8,128)} %copy-done.7), kind=kLoop, calls=%fused_computation.181 | loop fusion | flops 10223607 | bytes 37748772 | tf_op jit(solution)/shard_map/add | solution.py:44
  146.9 7.1 %fusion.3 = (f32[48,8,2048]{2,1,0:T(8,128)}, f32[48,8,2048]{2,1,0:T(8,128)}) fusion(f32[2,53,8,2048]{3,2,1,0:T(8,128)S(1)} %get-tuple-element.24, f32[48,8,2048]{2,1,0:T(8,128)} %copy-done.7, f32[2,53,8,2048]{3,2,1,0:T(8,128)S(1)} %get-tuple-element.25), kind=kLoop, calls=%fused_computation.47 | loop fusion | flops 12582912 | bytes 40894464 | tf_op jit(solution)/shard_map/add | solution.py:44
  154.1 7.1 %fusion.13 = (f32[48,8,2048]{2,1,0:T(8,128)}, f32[48,8,2048]{2,1,0:T(8,128)}) fusion(f32[2,53,8,2048]{3,2,1,0:T(8,128)S(1)} %get-tuple-element.24, f32[48,8,2048]{2,1,0:T(8,128)} %param.11, f32[2,53,8,2048]{3,2,1,0:T(8,128)S(1)} %get-tuple-element.25), kind=kLoop, calls=%fused_computation.60 | loop fusion | flops 12582912 | bytes 40894464 | tf_op jit(solution)/shard_map/add | solution.py:44
  161.1 8.3 %slice_multiply_fusion.1 = (f32[1,58,8,2048]{3,2,1,0:T(8,128)}, f32[1,58,8,2048]{3,2,1,0:T(8,128)}, f32[1,58,8,2048]{3,2,1,0:T(8,128)}) fusion(f32[2,58,8,2048]{3,2,1,0:T(8,128)} %copy-done.8), kind=kLoop, calls=%fused_computation.5 | loop fusion | flops 2850816 | bytes 19005440 | tf_op jit(solution)/shard_map/mul | solution.py:62
  169.4 51.9 %pmax.7 = f32[1]{0:T(128)} all-reduce(f32[1]{0:T(128)} %bitcast.12), channel_id=1, replica_groups=mesh['groups'=1,'rank'=32] {'rank'}, use_global_device_ids=true, to_apply=%region_1.2 | all-reduce | flops 1 | bytes 8 | tf_op jit(solution)/shard_map/pmax | solution.py:87
  221.3 41.3 %psum.7 = f32[8]{0:T(128)S(1)} all-reduce(f32[8]{0:T(128)S(1)} %get-tuple-element.23), channel_id=1, replica_groups=mesh['groups'=1,'rank'=32] {'rank'}, use_global_device_ids=true, to_apply=%region_3.4 | all-reduce | flops 8 | bytes 64 | tf_op jit(solution)/shard_map/psum | solution.py:88
  263.1 9.7 %fusion.28 = f32[48,8,2048]{2,1,0:T(8,128)} fusion(f32[1,52,8,2048]{3,2,1,0:T(8,128)} %get-tuple-element.19), kind=kLoop, calls=%fused_computation.108 | loop fusion | flops 3145728 | bytes 18874368 | tf_op jit(solution)/shard_map/add | solution.py:44
  272.8 3.5 fusion.25
  276.4 5.0 %fusion = f32[48,8,2048]{2,1,0:T(8,128)} fusion(f32[1,58,8,2048]{3,2,1,0:T(8,128)S(1)} %copy-done.4), kind=kLoop, calls=%fused_computation.14 | loop fusion | flops 7864320 | bytes 37748736 | tf_op jit(solution)/shard_map/add | solution.py:44
  281.4 5.1 %fusion.1 = f32[48,8,2048]{2,1,0:T(8,128)} fusion(f32[1,58,8,2048]{3,2,1,0:T(8,128)S(1)} %copy-done.3), kind=kLoop, calls=%fused_computation.25 | loop fusion | flops 7864320 | bytes 37748736 | tf_op jit(solution)/shard_map/add | solution.py:44
  286.5 5.1 %fusion.2 = f32[48,8,2048]{2,1,0:T(8,128)} fusion(f32[1,58,8,2048]{3,2,1,0:T(8,128)S(1)} %copy-done.2), kind=kLoop, calls=%fused_computation.36 | loop fusion | flops 7864320 | bytes 37748736 | tf_op jit(solution)/shard_map/add | solution.py:44
  291.6 5.3 %fusion.26 = (f32[48,8,2048]{2,1,0:T(8,128)}, f32[48,8,2048]{2,1,0:T(8,128)}) fusion(f32[1,52,8,2048]{3,2,1,0:T(8,128)S(1)} %copy-done.9, f32[1,52,8,2048]{3,2,1,0:T(8,128)S(1)} %copy-done.10), kind=kLoop, calls=%fused_computation.98 | loop fusion | flops 6291456 | bytes 37748736 | tf_op jit(solution)/shard_map/add | solution.py:44
  296.9 14.3 %fusion.23 = (f32[48,8,2048]{2,1,0:T(8,128)}, f32[48,8,2048]{2,1,0:T(8,128)}) fusion(f32[1,54,8,2048]{3,2,1,0:T(8,128)S(1)} %copy-done.5, f32[1,54,8,2048]{3,2,1,0:T(8,128)} %get-tuple-element.18), kind=kLoop, calls=%fused_computation.73 | loop fusion | flops 9437184 | bytes 50331648 | tf_op jit(solution)/shard_map/add | solution.py:44
  311.2 40.9 %multiply_divide_fusion.2 = f32[48,8,2048]{2,1,0:T(8,128)} fusion(f32[48,8,2048]{2,1,0:T(8,128)} %get-tuple-element.28, f32[48,8,2048]{2,1,0:T(8,128)} %get-tuple-element.29, f32[48,8,2048]{2,1,0:T(8,128)} %fusion.28, f32[48,8,2048]{2,1,0:T(8,128)} %get-tuple-element.12, f32[48,8,2048]{2,1,0:T(8,128)} %get-tuple-element.11), kind=kLoop, calls=%fused_computation.174 | loop fusion | flops 33816576 | bytes 18874368 | tf_op jit(solution)/shard_map/div | solution.py:36
  352.1 57.9 %multiply_divide_fusion.1 = f32[48,8,2048]{2,1,0:T(8,128)} fusion(f32[48,8,2048]{2,1,0:T(8,128)} %get-tuple-element.30, f32[48,8,2048]{2,1,0:T(8,128)} %get-tuple-element.31, f32[48,8,2048]{2,1,0:T(8,128)} %fusion.25, f32[48,8,2048]{2,1,0:T(8,128)} %get-tuple-element.10, f32[48,8,2048]{2,1,0:T(8,128)} %get-tuple-element.8), kind=kLoop, calls=%fused_computation.156 | loop fusion | flops 41680896 | bytes 18874368 | tf_op jit(solution)/shard_map/div | solution.py:36
  410.0 89.4 %multiply_divide_fusion = f32[48,8,2048]{2,1,0:T(8,128)} fusion(f32[48,8,2048]{2,1,0:T(8,128)} %fusion, f32[48,8,2048]{2,1,0:T(8,128)} %fusion.1, f32[48,8,2048]{2,1,0:T(8,128)} %fusion.2, f32[48,8,2048]{2,1,0:T(8,128)} %get-tuple-element.9, f32[48,8,2048]{2,1,0:T(8,128)} %get-tuple-element.7), kind=kLoop, calls=%fused_computation.120 | loop fusion | flops 57409536 | bytes 18874368 | tf_op jit(solution)/shard_map/div | solution.py:36
  (56 shorter events, 24.6 us)
Async XLA Ops:
  0.6 115.1 %copy-start = (f32[2048,256]{1,0:T(8,128)S(1)}, f32[2048,256]{1,0:T(8,128)}, u32[]{:S(2)}) copy-start(f32[2048,256]{1,0:T(8,128)} %param.8) | copy-start | bytes 6291460
  0.6 10.7 %copy-start.13 = (f32[8,1536]{1,0:T(8,128)S(1)}, f32[8,1536]{1,0:T(8,128)}, u32[]{:S(2)}) copy-start(f32[8,1536]{1,0:T(8,128)} %param.9) | copy-start | bytes 147460
  3.9 7.7 %copy-start.14 = (s32[8]{0:T(128)S(1)}, s32[8]{0:T(128)}, u32[]{:S(2)}) copy-start(s32[8]{0:T(128)} %param.10) | copy-start | bytes 100
  3.9 77.6 %all-to-all-start = ((f32[8,256,256]{1,0,2:T(8,128)}), f32[8,256,256]{1,0,2:T(8,128)}, u32[]{:S(2)}, u32[]{:S(2)}) async-start(f32[8,256,256]{1,0,2:T(8,128)} %copy.19), calls=%async_computation | async-start | bytes 4194304 | tf_op jit(solution)/shard_map/all_to_all | solution.py:77
  81.5 4.3 copy-start.12
  115.8 2.9 copy-start.11
  118.7 17.4 %copy-start.7 = (f32[48,8,2048]{2,1,0:T(8,128)}, f32[48,8,2048]{2,1,0:T(8,128)S(1)}, u32[]{:S(2)}) copy-start(f32[48,8,2048]{2,1,0:T(8,128)S(1)} %fusion.49) | copy-start | bytes 9437188
  118.8 4.6 collective-permute-start.1
  120.1 4.7 collective-permute-start
  125.6 6.2 %copy-start.8 = (f32[2,58,8,2048]{3,2,1,0:T(8,128)}, f32[2,58,8,2048]{3,2,1,0:T(8,128)S(1)}, u32[]{:S(2)}) copy-start(f32[2,58,8,2048]{3,2,1,0:T(8,128)S(1)} %pad_maximum_fusion) | copy-start | bytes 22806532
  263.1 9.7 %copy-start.6 = (f32[1,54,8,2048]{3,2,1,0:T(8,128)S(1)}, f32[1,54,8,2048]{3,2,1,0:T(8,128)}, u32[]{:S(2)}) copy-start(f32[1,54,8,2048]{3,2,1,0:T(8,128)} %get-tuple-element.16) | copy-start | bytes 10616836
  272.8 3.5 copy-start.4
  276.4 5.0 %copy-start.3 = (f32[1,58,8,2048]{3,2,1,0:T(8,128)S(1)}, f32[1,58,8,2048]{3,2,1,0:T(8,128)}, u32[]{:S(2)}) copy-start(f32[1,58,8,2048]{3,2,1,0:T(8,128)} %get-tuple-element.15) | copy-start | bytes 11403268
  281.4 5.1 %copy-start.2 = (f32[1,58,8,2048]{3,2,1,0:T(8,128)S(1)}, f32[1,58,8,2048]{3,2,1,0:T(8,128)}, u32[]{:S(2)}) copy-start(f32[1,58,8,2048]{3,2,1,0:T(8,128)} %get-tuple-element.13) | copy-start | bytes 11403268
  286.5 5.1 %copy-start.9 = (f32[1,52,8,2048]{3,2,1,0:T(8,128)S(1)}, f32[1,52,8,2048]{3,2,1,0:T(8,128)}, u32[]{:S(2)}) copy-start(f32[1,52,8,2048]{3,2,1,0:T(8,128)} %get-tuple-element.20) | copy-start | bytes 10223620
  286.5 5.1 %copy-start.10 = (f32[1,52,8,2048]{3,2,1,0:T(8,128)S(1)}, f32[1,52,8,2048]{3,2,1,0:T(8,128)}, u32[]{:S(2)}) copy-start(f32[1,52,8,2048]{3,2,1,0:T(8,128)} %get-tuple-element.21) | copy-start | bytes 10223620
  291.6 5.3 %copy-start.5 = (f32[1,54,8,2048]{3,2,1,0:T(8,128)S(1)}, f32[1,54,8,2048]{3,2,1,0:T(8,128)}, u32[]{:S(2)}) copy-start(f32[1,54,8,2048]{3,2,1,0:T(8,128)} %get-tuple-element.17) | copy-start | bytes 10616836
  410.0 89.4 %copy-start.1 = (f32[2048,256]{1,0:T(8,128)S(1)}, f32[2048,256]{1,0:T(8,128)}, u32[]{:S(2)}) copy-start(f32[2048,256]{1,0:T(8,128)} %param.8) | copy-start | bytes 6291460
where the time goes:
time: 508 us; the launch traced here: 500 us
  other arithmetic  281 us (55%)
  blocking collectives  182 us (36%)
  local copies, waits for them, and re-layouts  15.7 us (3%)
  starting transfers between devices  12 us (2%)
  matrix products  6.23 us (1%)
    div x3, other arithmetic, similarity(): return upper / lower  188 us
    add x10, other arithmetic, window_sums(): row_sums = row_sums + values[step_index:step_index + length]  69.3 us
    all_gather x1, blocking collectives, body(): all_picked = lax.all_gather(picked, 'rank', axis=0, tiled=True)  69.1 us
    pmax x1, blocking collectives, body(): max_error = lax.pmax(jnp.max(jnp.abs(misfit)).reshape(1), 'rank')  51.9 us
    psum x1, blocking collectives, body(): square_sums = lax.psum(jnp.sum(misfit * misfit, axis=(0, 2)), 'rank')  41.3 us
    all_to_all x1, blocking collectives, body(): lax.all_to_all(along_x, 'rank', split_axis=0, concat_axis=1, tiled=True)  19.7 us
    mul x3, other arithmetic, local_similarity(): target_rows * rebuilt_rows  16.8 us
  transfers between devices with their start and end apart: 3, of which 1 were waited for; matrix products, arithmetic and copies ran while one was open for 0% of the time, Pallas kernels for 0%

commit v1 on v0

v1 whole, which is shorter than its diff:
```python
import functools

import jax
import jax.numpy as jnp
from jax import lax
from jax.experimental import pallas as pl
from jax.experimental.pallas import tpu as pltpu
from jax.sharding import PartitionSpec as P

peak_value = 64.0
first_const = 0.01 * peak_value * (0.01 * peak_value)
second_const = 0.03 * peak_value * (0.03 * peak_value)
epsilon = 1e-06
windows = (5, 7, 11)
margin = 5
lanes = 128


def greet(me, count):
    barrier = pltpu.get_barrier_semaphore()

    def signal(step, carry):
        pl.semaphore_signal(barrier, inc=1, device_id={"rank": lax.rem(me + step, count)})
        return carry

    lax.fori_loop(1, count, signal, 0)
    pl.semaphore_wait(barrier, count - 1)


def exchange(me, count, source_at, received, send_sem, recv_sem):
    def copy_to(step):
        peer = lax.rem(me + step, count)
        return pltpu.make_async_remote_copy(
            src_ref=source_at(peer),
            dst_ref=received.at[me],
            send_sem=send_sem.at[step],
            recv_sem=recv_sem.at[step],
            device_id={"rank": peer},
        )

    def start(step, carry):
        copy_to(step).start()
        return carry

    def wait(step, carry):
        copy_to(step).wait()
        return carry

    lax.fori_loop(1, count, start, 0)
    return lambda: lax.fori_loop(1, count, wait, 0)


def sum_kernel(count, x_ref, out_ref, received, send_sem, recv_sem):
    me = lax.axis_index("rank")
    greet(me, count)
    finish = exchange(me, count, lambda peer: x_ref.at[peer], received, send_sem, recv_sem)
    received[me] = x_ref[me]
    finish()
    out_ref[...] = received[0]

    def add(index, carry):
        out_ref[...] += received[index]
        return carry

    lax.fori_loop(1, count, add, 0)


def sum_exchange(x):
    count = x.shape[0]
    return pl.pallas_call(
        functools.partial(sum_kernel, count),
        name="sum_exchange",
        out_shape=jax.ShapeDtypeStruct(x.shape[1:], x.dtype),
        in_specs=[pl.BlockSpec(memory_space=pltpu.VMEM)],
        out_specs=pl.BlockSpec(memory_space=pltpu.VMEM),
        scratch_shapes=[
            pltpu.VMEM(x.shape, x.dtype),
            pltpu.SemaphoreType.DMA((count,)),
            pltpu.SemaphoreType.DMA((count,)),
        ],
        compiler_params=pltpu.CompilerParams(collective_id=0, has_side_effects=True),
    )(x)


def swap_kernel(count, x_ref, out_ref, send_sem, recv_sem):
    me = lax.axis_index("rank")
    greet(me, count)
    finish = exchange(me, count, lambda peer: x_ref.at[peer], out_ref, send_sem, recv_sem)
    out_ref[me] = x_ref[me]
    finish()


def swap_exchange(x):
    count = x.shape[0]
    return pl.pallas_call(
        functools.partial(swap_kernel, count),
        name="swap_exchange",
        out_shape=jax.ShapeDtypeStruct(x.shape, x.dtype),
        in_specs=[pl.BlockSpec(memory_space=pltpu.VMEM)],
        out_specs=pl.BlockSpec(memory_space=pltpu.VMEM),
        scratch_shapes=[
            pltpu.SemaphoreType.DMA((count,)),
            pltpu.SemaphoreType.DMA((count,)),
        ],
        compiler_params=pltpu.CompilerParams(collective_id=1, has_side_effects=True),
    )(x)


def stats_kernel(count, cells, x_ref, error_ref, psnr_ref, received, send_sem, recv_sem):
    me = lax.axis_index("rank")
    greet(me, count)
    finish = exchange(me, count, lambda peer: x_ref, received, send_sem, recv_sem)
    received[me] = x_ref[...]
    finish()
    largest = received[0, 0]
    total = received[0, 1]

    def add(index, carry):
        return jnp.maximum(carry[0], received[index, 0]), carry[1] + received[index, 1]

    largest, total = lax.fori_loop(1, count, add, (largest, total))
    error_ref[...] = jnp.max(largest, keepdims=True)
    mean_square = jnp.sum(total, axis=1, keepdims=True) / cells
    psnr = 10.0 * (jnp.log(peak_value * peak_value / (mean_square + epsilon)) / jnp.log(10.0))
    psnr_ref[...] = psnr


def stats_exchange(x, count, cells):
    planes = x.shape[1]
    return pl.pallas_call(
        functools.partial(stats_kernel, count, cells),
        name="stats_exchange",
        out_shape=(
            jax.ShapeDtypeStruct((1, 1), x.dtype),
            jax.ShapeDtypeStruct((planes, 1), x.dtype),
        ),
        in_specs=[pl.BlockSpec(memory_space=pltpu.VMEM)],
        out_specs=(pl.BlockSpec(memory_space=pltpu.VMEM),) * 2,
        scratch_shapes=[
            pltpu.VMEM((count,) + x.shape, x.dtype),
            pltpu.SemaphoreType.DMA((count,)),
            pltpu.SemaphoreType.DMA((count,)),
        ],
        compiler_params=pltpu.CompilerParams(collective_id=2, has_side_effects=True),
    )(x)


def shifted(pieces, shift):
    lane = lax.broadcasted_iota(jnp.int32, pieces[0].shape, 1)
    turned = [pltpu.roll(piece, lanes - shift, 1) for piece in pieces]
    inside = lane < lanes - shift
    return [
        jnp.where(inside, turned[j], turned[(j + 1) % len(turned)]) for j in range(len(turned))
    ]


def added(left, right):
    return [a + b for a, b in zip(left, right)]


def across_sums(field):
    pairs = added(field, shifted(field, 1))
    fours = added(pairs, shifted(pairs, 2))
    five = added(fours, shifted(field, 4))
    seven = added(five, shifted(pairs, 5))
    eleven = added(seven, shifted(fours, 7))
    return five, seven, eleven


def down_sums(values, window, count):
    core = values[count - 1]
    for index in range(count, window):
        core = core + values[index]
    lefts = [core]
    for index in range(count - 2, -1, -1):
        lefts.insert(0, lefts[0] + values[index])
    results = [lefts[0]]
    right = None
    for index in range(1, count):
        item = values[window + index - 1]
        right = item if right is None else right + item
        results.append(lefts[index] + right)
    return results


def similarity(a, b, q, p, window):
    area = float(window * window)
    c1 = first_const * area * area
    c2 = second_const * area * area
    ab = a * b
    mm = a * a + b * b
    upper = (ab + 0.5 * c1) * (area * p - ab + 0.5 * c2) * 4.0
    lower = (mm + c1) * (area * q - mm + c2)
    return upper / lower


def map_kernel(length, rows_step, lag, low_ref, init_ref, high_ref, rebuilt_ref,
               five_ref, seven_ref, eleven_ref, stats_ref, ext, sums, sem):
    step = pl.program_id(0)
    extended = length + 2 * margin
    ring = (lag + 1) * rows_step
    pieces = init_ref.shape[2] // lanes
    planes = init_ref.shape[1]

    @pl.when(step == 0)
    def _():
        copies = [
            pltpu.make_async_copy(low_ref, ext.at[pl.ds(0, margin)], sem.at[0]),
            pltpu.make_async_copy(init_ref, ext.at[pl.ds(margin, length)], sem.at[1]),
            pltpu.make_async_copy(high_ref, ext.at[pl.ds(margin + length, margin)], sem.at[2]),
        ]
        for copy in copies:
            copy.start()
        for copy in copies:
            copy.wait()
        stats_ref[...] = jnp.zeros_like(stats_ref)

    def one_row(index, carry):
        row = step * rows_step + index
        slot = lax.rem(row, ring)
        zero = jnp.zeros((planes, lanes), jnp.float32)
        inits = [ext[row, :, j * lanes:(j + 1) * lanes] for j in range(pieces)]
        builts = [rebuilt_ref[row, :, j * lanes:(j + 1) * lanes] for j in range(pieces)]
        own = jnp.where((row >= margin) & (row < margin + length), 1.0, 0.0)
        largest, total = zero, zero
        for a, b in zip(inits, builts):
            misfit = a - b
            largest = jnp.maximum(largest, jnp.abs(misfit))
            total = total + misfit * misfit
        stats_ref[0] = jnp.maximum(stats_ref[0], largest * own)
        stats_ref[1] += total * own
        fields = (
            inits,
            builts,
            [a * a + b * b for a, b in zip(inits, builts)],
            [a * b for a, b in zip(inits, builts)],
        )
        for number, field in enumerate(fields):
            for which, values in enumerate(across_sums(field + [zero])):
                for j, value in enumerate(values):
                    sums[slot, which * 4 + number, :, j * lanes:(j + 1) * lanes] = value
        return carry

    lax.fori_loop(0, jnp.minimum(rows_step, extended - step * rows_step), one_row, 0)

    @pl.when(step >= lag)
    def _():
        base = (step - lag) * rows_step
        lane = lax.broadcasted_iota(jnp.int32, (planes, lanes), 1)
        for which, (window, out_ref) in enumerate(zip(windows, (five_ref, seven_ref, eleven_ref))):
            half = window // 2
            first = base + margin - half
            slots = [lax.rem(first + t, ring) for t in range(rows_step + window - 1)]

            def maps_at(j, which=which, window=window, slots=slots, half=half):
                place = pl.ds(pl.multiple_of(j * lanes, lanes), lanes)
                parts = []
                for number in range(4):
                    values = [sums[slot, which * 4 + number, :, place] for slot in slots]
                    results = []
                    done = 0
                    while done < rows_step:
                        count = min(4, rows_step - done)
                        results += down_sums(values[done:done + count + window - 1], window, count)
                        done += count
                    parts.append(results)
                return tuple(
                    pltpu.roll(similarity(a, b, q, p, window), half, 1)
                    for a, b, q, p in zip(*parts)
                )

            def column(j, before, out_ref=out_ref, maps_at=maps_at, half=half):
                now = maps_at(j)
                place = pl.ds(pl.multiple_of(j * lanes, lanes), lanes)
                for index in range(rows_step):
                    out_ref[index, :, place] = jnp.where(lane < half, before[index], now[index])
                return now

            lax.fori_loop(0, pieces, column, maps_at(pieces))


def similarity_maps(low, initial, high, rebuilt):
    length, planes, across = initial.shape
    rows_step = max(size for size in range(1, 9) if length % size == 0)
    lag = -(-2 * margin // rows_step)
    out = jax.ShapeDtypeStruct(initial.shape, jnp.float32)
    out_spec = pl.BlockSpec((rows_step, planes, across), lambda s: (jnp.maximum(s - lag, 0), 0, 0))
    whole = pl.BlockSpec(memory_space=pltpu.VMEM)
    extended = length + 2 * margin
    return pl.pallas_call(
        functools.partial(map_kernel, length, rows_step, lag),
        name="similarity_maps",
        grid=(length // rows_step + lag,),
        out_shape=(out, out, out, jax.ShapeDtypeStruct((2, planes, lanes), jnp.float32)),
        in_specs=[pl.BlockSpec(memory_space=pl.ANY)] * 3 + [whole],
        out_specs=(out_spec, out_spec, out_spec, whole),
        scratch_shapes=[
            pltpu.VMEM((extended, planes, across), jnp.float32),
            pltpu.VMEM(((lag + 1) * rows_step, 12, planes, across + lanes), jnp.float32),
            pltpu.SemaphoreType.DMA((3,)),
        ],
        compiler_params=pltpu.CompilerParams(
            dimension_semantics=("arbitrary",), vmem_limit_bytes=60 * 1024 * 1024
        ),
    )(low, initial, high, rebuilt)


def body(core, x_factor, y_factor, z_factor, offsets, initial):
    exact = lax.Precision.HIGHEST
    count = lax.axis_size("rank")
    planes = offsets.shape[0]
    along, rank = x_factor.shape
    across = y_factor.shape[0]
    length = initial.shape[0]
    forward = [(i, i + 1) for i in range(count - 1)]
    backward = [(target, source) for source, target in forward]
    low = lax.ppermute(initial[length - margin:], "rank", forward)
    high = lax.ppermute(initial[:margin], "rank", backward)

    parts = count // planes
    width = rank // parts
    picked = jnp.take(z_factor, offsets, axis=1)
    partial = jnp.einsum("kab,kp->pba", core, picked, precision=exact)
    owned = sum_exchange(partial.reshape(count, width, rank))

    pack = lanes // width
    extended = length + 2 * margin
    each = -(-extended // pack)
    padded = jnp.pad(x_factor, ((margin, margin + each * pack), (0, 0)))
    blocks = jnp.stack([padded[d * length:d * length + each * pack] for d in range(count)])
    expanded = jnp.einsum("dxa,ba->dxb", blocks, owned, precision=exact)
    packed = (
        expanded.reshape(count, pack, each, width)
        .transpose(0, 2, 1, 3)
        .reshape(count, each, pack * width)
    )
    arrived = swap_exchange(packed)
    rows = (
        arrived.reshape(planes, parts, each, pack, width)
        .transpose(3, 2, 0, 1, 4)
        .reshape(pack * each, planes, rank)[:extended]
    )
    rebuilt = jnp.einsum("xpb,yb->xpy", rows, y_factor, precision=exact)
    five, seven, eleven, stats = similarity_maps(low, initial, high, rebuilt)
    error, psnr = stats_exchange(stats, count, float(along * across))
    return error.reshape(1), psnr.reshape(planes), five, seven, eleven


def solution(mesh):
    placed = (
        P("rank", "groups", None),
        P("groups", None),
        P("groups", None),
        P("rank", "groups"),
        P("groups"),
        P("rank", "groups", None),
    )
    return jax.shard_map(
        body,
        mesh=mesh,
        in_specs=placed,
        out_specs=(
            P("groups"),
            P("groups"),
            P("rank", "groups", None),
            P("rank", "groups", None),
            P("rank", "groups", None),
        ),
        check_vma=False,
    )
```

time: 508 us -> 208 us (0.41); the launches traced: 500 us -> 207 us
  other arithmetic: 281 us -> 2.64 us
  blocking collectives: 182 us -> 0 us
  Pallas kernels: 0 us -> 165 us
  starting transfers between devices: 12 us -> 5.06 us
  matrix products: 6.23 us -> 12.7 us
    div x3 -> x0, other arithmetic: 188 us -> none  [similarity(): return upper / lower]
    pallas_call x0 -> x4, Pallas kernels: none -> 165 us  [the longest x1 75.8 us: similarity_maps(): pl.pallas_call(functools.partial(map_kernel, length, rows_step, lag), nam...]
    add x10 -> x0, other arithmetic: 69.3 us -> none  [window_sums(): row_sums = row_sums + values[step_index:step_index + length]]
    all_gather x1 -> x0, blocking collectives: 69.1 us -> none  [body(): all_picked = lax.all_gather(picked, 'rank', axis=0, tiled=True)]
    pmax x1 -> x0, blocking collectives: 51.9 us -> none  [body(): max_error = lax.pmax(jnp.max(jnp.abs(misfit)).reshape(1), 'rank')]
    psum x1 -> x0, blocking collectives: 41.3 us -> none  [body(): square_sums = lax.psum(jnp.sum(misfit * misfit, axis=(0, 2)), 'rank')]
    all_to_all x1 -> x0, blocking collectives: 19.7 us -> none  [body(): lax.all_to_all(along_x, 'rank', split_axis=0, concat_axis=1, tiled=True)]
    mul x4 -> x0, other arithmetic: 17.3 us -> none  [the longest x3 16.8 us: local_similarity(): target_rows * rebuilt_rows]
  transfers between devices with their start and end apart: 3 -> 2, of which waited for: 1 -> 0; matrix products, arithmetic and copies ran while one was open for 0% -> 15% of each run, Pallas kernels for 0% -> 36%
where the time goes in v1:
time: 208 us; the launch traced here: 207 us
  Pallas kernels  165 us (79%)
  local copies, waits for them, and re-layouts  19.4 us (9%)
  matrix products  12.7 us (6%)
  starting transfers between devices  5.06 us (2%)
  between operations  2.79 us (1%)
  other arithmetic  2.64 us (1%)
    pallas_call x1, Pallas kernels, similarity_maps(): pl.pallas_call(functools.partial(map_kernel, length, rows_step, lag), nam...  75.8 us
    pallas_call x1, Pallas kernels, sum_exchange(): pl.pallas_call(functools.partial(sum_kernel, count), name='sum_exchange',...  47.8 us
    pallas_call x1, Pallas kernels, swap_exchange(): pl.pallas_call(functools.partial(swap_kernel, count), name='swap_exchange...  26.4 us
    pallas_call x1, Pallas kernels, stats_exchange(): pl.pallas_call(functools.partial(stats_kernel, count, cells), name='stats...  14.5 us
    unnamed x38, local copies, waits for them, and re-layouts  6.33 us
    dot_general x1, matrix products, body(): partial = jnp.einsum('kab,kp->pba', core, picked, precision=exact)  5.75 us
    dot_general x1, matrix products, body(): rebuilt = jnp.einsum('xpb,yb->xpy', rows, y_factor, precision=exact)  5.09 us
  transfers between devices with their start and end apart: 2, of which 0 were waited for; matrix products, arithmetic and copies ran while one was open for 15% of the time, Pallas kernels for 36%

profile of v1, /device:TPU:0, one launch (start us, length us, event | category | flops | bytes accessed | tf_op | source)
XLA Modules:
  0.0 207.1 jit_solution(9727902367766811541)
XLA Ops:
  0.6 2.1 %fusion.18 = (f32[5,8,2048]{2,1,0:T(8,128)}, f32[5,8,2048]{2,1,0:T(8,128)}) fusion(f32[48,8,2048]{2,1,0:T(8,128)} %init_ref.1), kind=kLoop, calls=%fused_computation.52 | loop fusion | bytes 1310720 | tf_op jit(solution)/shard_map/slice | solution.py:318
  2.8 1.3 collective-permute-start.1
  4.1 3.8 %collective-permute-start = (f32[5,8,2048]{2,1,0:T(8,128)}, f32[5,8,2048]{2,1,0:T(8,128)}, u32[]{:S(2)}, u32[]{:S(2)}) collective-permute-start(f32[5,8,2048]{2,1,0:T(8,128)} %get-tuple-element.18), channel_id=1, source_target_pairs={{0,1},{1,2},{2,3},{3,4},{4,5},{5,6},{6,7},{7,8},{8,9},{9,10},{10,1... | collective-permute-start | bytes 983048 | tf_op jit(solution)/shard_map/ppermute | solution.py:317
  7.8 0.7 compare_and_fusion
  9.2 1.1 copy.23
  10.8 5.8 %fusion.4 = f32[8,256,256]{1,0,2:T(8,128)} fusion(f32[8,256,256]{2,1,0:T(8,128)} %param.6, f32[8,8]{1,0:T(8,128)S(1)} %gather_fusion, pred[8]{0:T(512)(128)(4,1)S(1)} %compare_and_fusion), kind=kOutput, calls=%fused_computation.5 | convolution fusion | flops 50331712 | bytes 4194568 | tf_op jit(solution)/shard_map/kab,kp->pba/dot_general | solution.py:323
  16.5 2.9 %copy.25 = f32[8,256,256]{2,1,0:T(8,128)} copy(f32[8,256,256]{1,0,2:T(8,128)} %fusion.4) | data formatting | bytes 4194304 | tf_op jit(solution)/shard_map/kab,kp->pba/transpose | solution.py:323
  19.4 47.8 %sum_exchange.1 = f32[64,256]{1,0:T(8,128)} custom-call(f32[32,64,256]{2,1,0:T(8,128)} %bitcast.89), custom_call_target="tpu_custom_call" | custom-call | tf_op jit(solution)/shard_map/sum_exchange/pallas_call | solution.py:70
  67.3 1.0 fusion.8
  68.3 0.9 constant_dynamic-update-slice_fusion.29
  69.1 0.9 constant_dynamic-update-slice_fusion.28
  70.0 0.9 constant_dynamic-update-slice_fusion.27
  70.9 0.9 constant_dynamic-update-slice_fusion.26
  72.8 1.8 fusion.11
  75.2 0.7 copy.31
  75.9 1.4 reshape.55.x_ref
  77.3 26.4 %swap_exchange.1 = f32[32,29,128]{2,1,0:T(8,128)} custom-call(f32[32,29,128]{2,1,0:T(8,128)} %reshape.55.x_ref), custom_call_target="tpu_custom_call" | custom-call | tf_op jit(solution)/shard_map/swap_exchange/pallas_call | solution.py:95
  103.7 1.3 copy.29
  105.6 1.2 copy.30
  106.7 1.7 reshape.40
  108.5 5.1 %fusion.rebuilt_ref = f32[58,8,2048]{2,1,0:T(8,128)} fusion(f32[58,8,256]{2,1,0:T(8,128)S(1)} %reshape.40, f32[2048,256]{1,0:T(8,128)S(1)} %copy-done), kind=kOutput, calls=%fused_computation.1 | convolution fusion | flops 2919235584 | bytes 6373376 | tf_op jit(solution)/shard_map/xpb,yb->xpy/dot_general | solution.py:343
  113.6 75.8 %similarity_maps.1 = (f32[48,8,2048]{2,1,0:T(8,128)}, f32[48,8,2048]{2,1,0:T(8,128)}, f32[48,8,2048]{2,1,0:T(8,128)}, f32[2,8,128]{2,1,0:T(8,128)}) custom-call(f32[5,8,2048]{2,1,0:T(8,128)} %collective-permute-done.low_ref, f32[48,8,2048]{2,1,0:T(8,128)} %init_ref.1, f32[5,8,2048]{2,1,0:T(8,128)} %collective-permute-done.1.high_ref, ...), custom_call_target="tpu_custom_call" | custom-call | tf_op jit(solution)/shard_map/similarity_maps/pallas_call | solution.py:290
  189.5 14.5 %stats_exchange.1 = (f32[1,1]{1,0:T(1,128)}, f32[8,1]{1,0:T(8,128)}) custom-call(f32[2,8,128]{2,1,0:T(8,128)} %get-tuple-element.11.x_ref), custom_call_target="tpu_custom_call" | custom-call | tf_op jit(solution)/shard_map/stats_exchange/pallas_call | solution.py:130
  203.9 1.3 reduce
  (40 shorter events, 3.1 us)
Async XLA Ops:
  0.6 107.9 %copy-start = (f32[2048,256]{1,0:T(8,128)S(1)}, f32[2048,256]{1,0:T(8,128)}, u32[]{:S(2)}) copy-start(f32[2048,256]{1,0:T(8,128)} %param.8) | copy-start | bytes 6291460
  2.8 110.8 %collective-permute-start.1 = (f32[5,8,2048]{2,1,0:T(8,128)}, f32[5,8,2048]{2,1,0:T(8,128)}, u32[]{:S(2)}, u32[]{:S(2)}) collective-permute-start(f32[5,8,2048]{2,1,0:T(8,128)} %get-tuple-element.17), channel_id=1, source_target_pairs={{1,0},{2,1},{3,2},{4,3},{5,4},{6,5},{7,6},{8,7},{9,8},{10,9},{11,1... | collective-permute-start | bytes 983048 | tf_op jit(solution)/shard_map/ppermute | solution.py:318
  4.1 109.5 %collective-permute-start = (f32[5,8,2048]{2,1,0:T(8,128)}, f32[5,8,2048]{2,1,0:T(8,128)}, u32[]{:S(2)}, u32[]{:S(2)}) collective-permute-start(f32[5,8,2048]{2,1,0:T(8,128)} %get-tuple-element.18), channel_id=1, source_target_pairs={{0,1},{1,2},{2,3},{3,4},{4,5},{5,6},{6,7},{7,8},{8,9},{9,10},{10,1... | collective-permute-start | bytes 983048 | tf_op jit(solution)/shard_map/ppermute | solution.py:317
  67.3 4.5 %copy-start.1 = (f32[1536,256]{1,0:T(8,128)S(1)}, f32[1536,256]{1,0:T(8,128)}, u32[]{:S(2)}) copy-start(f32[1536,256]{1,0:T(8,128)} %param.7) | copy-start | bytes 4718596
  71.9 0.8 copy-start.2

commit v2 on v1

--- a/solution.py
+++ b/solution.py
@@ -82,20 +82,23 @@
     )(x)
 
 
-def swap_kernel(count, x_ref, out_ref, send_sem, recv_sem):
+def swap_kernel(count, stride, each, x_ref, out_ref, send_sem, recv_sem):
     me = lax.axis_index("rank")
+
+    def source_at(peer):
+        return x_ref.at[pl.ds(pl.multiple_of(peer * stride, 8), each)]
+
     greet(me, count)
-    finish = exchange(me, count, lambda peer: x_ref.at[peer], out_ref, send_sem, recv_sem)
-    out_ref[me] = x_ref[me]
+    finish = exchange(me, count, source_at, out_ref, send_sem, recv_sem)
+    out_ref[me] = x_ref[pl.ds(pl.multiple_of(me * stride, 8), each)]
     finish()
 
 
-def swap_exchange(x):
-    count = x.shape[0]
+def swap_exchange(x, count, stride, each):
     return pl.pallas_call(
-        functools.partial(swap_kernel, count),
+        functools.partial(swap_kernel, count, stride, each),
         name="swap_exchange",
-        out_shape=jax.ShapeDtypeStruct(x.shape, x.dtype),
+        out_shape=jax.ShapeDtypeStruct((count, each) + x.shape[1:], x.dtype),
         in_specs=[pl.BlockSpec(memory_space=pltpu.VMEM)],
         out_specs=pl.BlockSpec(memory_space=pltpu.VMEM),
         scratch_shapes=[
@@ -143,28 +146,6 @@
         ],
         compiler_params=pltpu.CompilerParams(collective_id=2, has_side_effects=True),
     )(x)
-
-
-def shifted(pieces, shift):
-    lane = lax.broadcasted_iota(jnp.int32, pieces[0].shape, 1)
-    turned = [pltpu.roll(piece, lanes - shift, 1) for piece in pieces]
-    inside = lane < lanes - shift
-    return [
-        jnp.where(inside, turned[j], turned[(j + 1) % len(turned)]) for j in range(len(turned))
-    ]
-
-
-def added(left, right):
-    return [a + b for a, b in zip(left, right)]
-
-
-def across_sums(field):
-    pairs = added(field, shifted(field, 1))
-    fours = added(pairs, shifted(pairs, 2))
-    five = added(fours, shifted(field, 4))
-    seven = added(five, shifted(pairs, 5))
-    eleven = added(seven, shifted(fours, 7))
-    return five, seven, eleven
 
 
 def down_sums(values, window, count):
@@ -195,7 +176,7 @@
 
 
 def map_kernel(length, rows_step, lag, low_ref, init_ref, high_ref, rebuilt_ref,
-               five_ref, seven_ref, eleven_ref, stats_ref, ext, sums, sem):
+               five_ref, seven_ref, eleven_ref, stats_ref, ext, sums, fields, pairs, raw, sem):
     step = pl.program_id(0)
     extended = length + 2 * margin
     ring = (lag + 1) * rows_step
@@ -215,74 +196,102 @@
             copy.wait()
         stats_ref[...] = jnp.zeros_like(stats_ref)
 
+    wide = pieces * planes
+
+    def turned(values):
+        lane = lax.broadcasted_iota(jnp.int32, (8, wide), 1)
+        inner = jnp.concatenate(values, axis=0).T
+        rows = [inner[8 * v:8 * v + 8] for v in range(lanes // 8)]
+        above = jnp.where(lane < planes, 0.0, pltpu.roll(rows[-1], planes, 1))
+        below = jnp.where(lane < wide - planes, pltpu.roll(rows[0], wide - planes, 1), 0.0)
+        return [above] + rows + [below]
+
     def one_row(index, carry):
         row = step * rows_step + index
-        slot = lax.rem(row, ring)
-        zero = jnp.zeros((planes, lanes), jnp.float32)
-        inits = [ext[row, :, j * lanes:(j + 1) * lanes] for j in range(pieces)]
-        builts = [rebuilt_ref[row, :, j * lanes:(j + 1) * lanes] for j in range(pieces)]
+        slot = lax.rem(row + ring - 1, ring)
+        for number in range(4):
+            for v in range(lanes // 8 + 2):
+                pairs[number, 8 * v:8 * v + 8] = (
+                    fields[number, 8 * v:8 * v + 8] + fields[number, 8 * v + 1:8 * v + 9]
+                )
+            for v in range(lanes // 8):
+                def pair(offset, v=v, number=number):
+                    return pairs[number, 8 * v + 8 + offset:8 * v + 16 + offset]
+
+                def single(offset, v=v, number=number):
+                    return fields[number, 8 * v + 8 + offset:8 * v + 16 + offset]
+
+                five = pair(-2) + pair(0) + single(2)
+                seven = five + (single(-3) + single(3))
+                eleven = seven + (pair(-5) + pair(4))
+                sums[slot, number, 8 * v:8 * v + 8] = five
+                sums[slot, 4 + number, 8 * v:8 * v + 8] = seven
+                sums[slot, 8 + number, 8 * v:8 * v + 8] = eleven
+        source = jnp.minimum(row, extended - 1)
         own = jnp.where((row >= margin) & (row < margin + length), 1.0, 0.0)
-        largest, total = zero, zero
+        inits = [ext[source, :, j * lanes:(j + 1) * lanes] for j in range(pieces)]
+        builts = [rebuilt_ref[source, :, j * lanes:(j + 1) * lanes] for j in range(pieces)]
+        largest = jnp.zeros((planes, lanes), jnp.float32)
+        total = largest
         for a, b in zip(inits, builts):
             misfit = a - b
             largest = jnp.maximum(largest, jnp.abs(misfit))
             total = total + misfit * misfit
         stats_ref[0] = jnp.maximum(stats_ref[0], largest * own)
         stats_ref[1] += total * own
-        fields = (
-            inits,
-            builts,
-            [a * a + b * b for a, b in zip(inits, builts)],
-            [a * b for a, b in zip(inits, builts)],
-        )
-        for number, field in enumerate(fields):
-            for which, values in enumerate(across_sums(field + [zero])):
-                for j, value in enumerate(values):
-                    sums[slot, which * 4 + number, :, j * lanes:(j + 1) * lanes] = value
-        return carry
-
-    lax.fori_loop(0, jnp.minimum(rows_step, extended - step * rows_step), one_row, 0)
+        for v, (a, b) in enumerate(zip(turned(inits), turned(builts))):
+            place = slice(8 * v, 8 * v + 8)
+            fields[0, place] = a
+            fields[1, place] = b
+            fields[2, place] = a * a + b * b
+            fields[3, place] = a * b
+        return carry
+
+    lax.fori_loop(0, jnp.minimum(rows_step, extended + 1 - step * rows_step), one_row, 0)
 
     @pl.when(step >= lag)
     def _():
         base = (step - lag) * rows_step
-        lane = lax.broadcasted_iota(jnp.int32, (planes, lanes), 1)
         for which, (window, out_ref) in enumerate(zip(windows, (five_ref, seven_ref, eleven_ref))):
-            half = window // 2
-            first = base + margin - half
+            first = base + margin - window // 2
             slots = [lax.rem(first + t, ring) for t in range(rows_step + window - 1)]
 
-            def maps_at(j, which=which, window=window, slots=slots, half=half):
-                place = pl.ds(pl.multiple_of(j * lanes, lanes), lanes)
-                parts = []
-                for number in range(4):
-                    values = [sums[slot, which * 4 + number, :, place] for slot in slots]
-                    results = []
-                    done = 0
-                    while done < rows_step:
-                        count = min(4, rows_step - done)
-                        results += down_sums(values[done:done + count + window - 1], window, count)
-                        done += count
-                    parts.append(results)
-                return tuple(
-                    pltpu.roll(similarity(a, b, q, p, window), half, 1)
-                    for a, b, q, p in zip(*parts)
-                )
-
-            def column(j, before, out_ref=out_ref, maps_at=maps_at, half=half):
-                now = maps_at(j)
-                place = pl.ds(pl.multiple_of(j * lanes, lanes), lanes)
-                for index in range(rows_step):
-                    out_ref[index, :, place] = jnp.where(lane < half, before[index], now[index])
-                return now
-
-            lax.fori_loop(0, pieces, column, maps_at(pieces))
+            def maps_at(j, which=which, window=window, slots=slots):
+                place = pl.ds(pl.multiple_of(j * 8, 8), 8)
+                done = 0
+                while done < rows_step:
+                    count = min(4, rows_step - done)
+                    parts = []
+                    for number in range(4):
+                        values = [
+                            sums[slot, which * 4 + number, place]
+                            for slot in slots[done:done + count + window - 1]
+                        ]
+                        parts.append(down_sums(values, window, count))
+                    for index, (a, b, q, p) in enumerate(zip(*parts)):
+                        raw[which, done + index, place] = similarity(a, b, q, p, window)
+                    done += count
+
+            def columns(pair, carry, maps_at=maps_at):
+                maps_at(2 * pair)
+                maps_at(2 * pair + 1)
+                return carry
+
+            lax.fori_loop(0, lanes // 16, columns, 0)
+        for which, out_ref in enumerate((five_ref, seven_ref, eleven_ref)):
+            for index in range(rows_step):
+                back = raw[which, index].T
+                for j in range(pieces):
+                    out_ref[index, :, j * lanes:(j + 1) * lanes] = back[
+                        j * planes:(j + 1) * planes
+                    ]
 
 
 def similarity_maps(low, initial, high, rebuilt):
     length, planes, across = initial.shape
     rows_step = max(size for size in range(1, 9) if length % size == 0)
-    lag = -(-2 * margin // rows_step)
+    lag = -(-(2 * margin + 1) // rows_step)
+    wide = planes * across // lanes
     out = jax.ShapeDtypeStruct(initial.shape, jnp.float32)
     out_spec = pl.BlockSpec((rows_step, planes, across), lambda s: (jnp.maximum(s - lag, 0), 0, 0))
     whole = pl.BlockSpec(memory_space=pltpu.VMEM)
@@ -296,7 +305,10 @@
         out_specs=(out_spec, out_spec, out_spec, whole),
         scratch_shapes=[
             pltpu.VMEM((extended, planes, across), jnp.float32),
-            pltpu.VMEM(((lag + 1) * rows_step, 12, planes, across + lanes), jnp.float32),
+            pltpu.VMEM(((lag + 1) * rows_step, 12, lanes, wide), jnp.float32),
+            pltpu.VMEM((4, lanes + 24, wide), jnp.float32),
+            pltpu.VMEM((4, lanes + 24, wide), jnp.float32),
+            pltpu.VMEM((3, rows_step, lanes, wide), jnp.float32),
             pltpu.SemaphoreType.DMA((3,)),
         ],
         compiler_params=pltpu.CompilerParams(
@@ -325,20 +337,31 @@
 
     pack = lanes // width
     extended = length + 2 * margin
-    each = -(-extended // pack)
-    padded = jnp.pad(x_factor, ((margin, margin + each * pack), (0, 0)))
-    blocks = jnp.stack([padded[d * length:d * length + each * pack] for d in range(count)])
-    expanded = jnp.einsum("dxa,ba->dxb", blocks, owned, precision=exact)
-    packed = (
-        expanded.reshape(count, pack, each, width)
-        .transpose(0, 2, 1, 3)
-        .reshape(count, each, pack * width)
+    before = -(-margin // pack) * pack
+    each = -(-(before - margin + extended) // (8 * pack)) * 8
+    if length % (8 * pack) == 0:
+        stride = length // pack
+        last = (count - 1) * length + each * pack - before - along
+        blocks = jnp.pad(x_factor, ((before, last), (0, 0)))
+    else:
+        stride = each
+        padded = jnp.pad(x_factor, ((before, each * pack), (0, 0)))
+        blocks = jnp.concatenate(
+            [padded[d * length:d * length + each * pack] for d in range(count)]
+        )
+    blocks = blocks.reshape(-1, pack, rank)
+    expanded = jnp.concatenate(
+        [
+            jnp.einsum("xa,ba->xb", blocks[:, h], owned, precision=exact)
+            for h in range(pack)
+        ],
+        axis=1,
     )
-    arrived = swap_exchange(packed)
+    arrived = swap_exchange(expanded, count, stride, each)
     rows = (
         arrived.reshape(planes, parts, each, pack, width)
-        .transpose(3, 2, 0, 1, 4)
-        .reshape(pack * each, planes, rank)[:extended]
+        .transpose(2, 3, 0, 1, 4)
+        .reshape(each * pack, planes, rank)[before - margin:before - margin + extended]
     )
     rebuilt = jnp.einsum("xpb,yb->xpy", rows, y_factor, precision=exact)
     five, seven, eleven, stats = similarity_maps(low, initial, high, rebuilt)

time: 208 us -> 173 us (0.83)
  Pallas kernels: 165 us -> 124 us
  local copies, waits for them, and re-layouts: 19.4 us -> 23.5 us
    pallas_call x1, Pallas kernels: 75.8 us -> 34.1 us  [similarity_maps(): pl.pallas_call(functools.partial(map_kernel, length, rows_step, lag), nam...]
    unnamed x38 -> x3, local copies, waits for them, and re-layouts: 6.33 us -> 1.97 us
    slice x0 -> x1, local copies, waits for them, and re-layouts: none -> 4.14 us  [body(): blocks[:, h]]
    pad x0 -> x1, local copies, waits for them, and re-layouts: none -> 2.66 us  [body(): blocks = jnp.pad(x_factor, ((before, last), (0, 0)))]
    reshape x4 -> x3, local copies, waits for them, and re-layouts: 4.4 us -> 6.51 us  [the longest x1 3.02 us: body(): blocks = blocks.reshape(-1, pack, rank)]
  transfers between devices with their start and end apart: 2 -> 2, of which waited for: 0 -> 0; matrix products, arithmetic and copies ran while one was open for 15% -> 22% of each run, Pallas kernels for 36% -> 43%
where the time goes in v2:
time: 173 us
  Pallas kernels  124 us (72%)
  local copies, waits for them, and re-layouts  23.5 us (14%)
  matrix products  14.4 us (8%)
  starting transfers between devices  5.06 us (3%)
  other arithmetic  3.56 us (2%)
  between operations  2.41 us (1%)
    pallas_call x1, Pallas kernels, sum_exchange(): pl.pallas_call(functools.partial(sum_kernel, count), name='sum_exchange',...  47.8 us
    pallas_call x1, Pallas kernels, similarity_maps(): pl.pallas_call(functools.partial(map_kernel, length, rows_step, lag), nam...  34.1 us
    pallas_call x1, Pallas kernels, swap_exchange(): pl.pallas_call(functools.partial(swap_kernel, count, stride, each), name=...  27.1 us
    pallas_call x1, Pallas kernels, stats_exchange(): pl.pallas_call(functools.partial(stats_kernel, count, cells), name='stats...  14.7 us
    dot_general x1, matrix products, body(): partial = jnp.einsum('kab,kp->pba', core, picked, precision=exact)  5.75 us
    dot_general x1, matrix products, body(): rebuilt = jnp.einsum('xpb,yb->xpy', rows, y_factor, precision=exact)  5.07 us
    slice x1, local copies, waits for them, and re-layouts, body(): blocks[:, h]  4.14 us
    ppermute x1, starting transfers between devices, body(): low = lax.ppermute(initial[length - margin:], 'rank', forward)  3.78 us
  transfers between devices with their start and end apart: 2, of which 0 were waited for; matrix products, arithmetic and copies ran while one was open for 22% of the time, Pallas kernels for 43%

profile of v2, /device:TPU:0, one launch (start us, length us, event | category | flops | bytes accessed | tf_op | source)
XLA Modules:
  0.0 172.7 jit_solution(4329707675410311866)
XLA Ops:
  0.6 2.0 %fusion.18 = (f32[5,8,2048]{2,1,0:T(8,128)}, f32[5,8,2048]{2,1,0:T(8,128)S(1)}) fusion(f32[48,8,2048]{2,1,0:T(8,128)} %init_ref.1), kind=kLoop, calls=%fused_computation.21 | loop fusion | bytes 1310720 | tf_op jit(solution)/shard_map/slice | solution.py:330
  2.7 1.3 collective-permute-start.1
  4.0 3.8 %collective-permute-start = (f32[5,8,2048]{2,1,0:T(8,128)S(1)}, f32[5,8,2048]{2,1,0:T(8,128)}, u32[]{:S(2)}, u32[]{:S(2)}) collective-permute-start(f32[5,8,2048]{2,1,0:T(8,128)S(1)} %get-tuple-element.18), channel_id=1, source_target_pairs={{0,1},{1,2},{2,3},{3,4},{4,5},{5,6},{6,7},{7,8},{8,9},{9,10},{10,1... | collective-permute-start | bytes 983048 | tf_op jit(solution)/shard_map/ppermute | solution.py:329
  7.7 0.7 compare_and_fusion
  8.4 0.7 compare_select_fusion
  9.1 2.0 %copy.17 = f32[8,1536]{0,1:T(8,128)} copy(f32[8,1536]{1,0:T(8,128)} %param.9) | data formatting | bytes 98304 | tf_op args[3]
  11.0 2.7 %pad.4 = f32[1552,256]{1,0:T(8,128)} pad(f32[1536,256]{1,0:T(8,128)} %param.7, f32[]{:T(128)} %constant.14.clone.1), padding=6_10x0_0 | pad | bytes 3162116 | tf_op jit(solution)/shard_map/jit(_pad)/pad | solution.py:345
  13.7 3.0 %reshape.33 = f32[776,2,256]{2,1,0:T(2,128)} reshape(f32[1552,256]{1,0:T(8,128)} %pad.4) | data formatting | bytes 3178496 | tf_op jit(solution)/shard_map/reshape | solution.py:352
  16.7 4.1 %fusion.19 = (f32[776,1,256]{2,1,0:T(1,128)S(1)}, f32[776,1,256]{2,1,0:T(1,128)}) fusion(f32[776,2,256]{2,1,0:T(2,128)} %reshape.33), kind=kLoop, calls=%fused_computation.22 | loop fusion | bytes 3178496 | tf_op jit(solution)/shard_map/slice | solution.py:355
  20.8 1.7 gather_fusion
  22.5 5.8 %fusion.4 = f32[8,256,256]{1,0,2:T(8,128)} fusion(f32[8,256,256]{2,1,0:T(8,128)} %param.6, f32[8,8]{1,0:T(8,128)S(1)} %gather_fusion, pred[8]{0:T(512)(128)(4,1)S(1)} %compare_and_fusion), kind=kOutput, calls=%fused_computation.5 | convolution fusion | flops 50331712 | bytes 4194568 | tf_op jit(solution)/shard_map/kab,kp->pba/dot_general | solution.py:335
  28.3 2.9 %copy.19 = f32[8,256,256]{2,1,0:T(8,128)} copy(f32[8,256,256]{1,0,2:T(8,128)} %fusion.4) | data formatting | bytes 4194304 | tf_op jit(solution)/shard_map/kab,kp->pba/transpose | solution.py:335
  31.2 47.8 %sum_exchange.1 = f32[64,256]{1,0:T(8,128)} custom-call(f32[32,64,256]{2,1,0:T(8,128)} %bitcast.20), custom_call_target="tpu_custom_call" | custom-call | tf_op jit(solution)/shard_map/sum_exchange/pallas_call | solution.py:70
  79.0 1.9 %fusion.7 = f32[776,64]{1,0:T(8,128)S(1)} fusion(f32[64,256]{1,0:T(8,128)} %sum_exchange.1, f32[776,1,256]{2,1,0:T(1,128)} %get-tuple-element.20), kind=kOutput, calls=%fused_computation.6 | convolution fusion | flops 152567808 | bytes 1058816 | tf_op jit(solution)/shard_map/xa,ba->xb/dot_general | solution.py:355
  80.9 1.6 fusion.10
  82.6 0.9 pad_maximum_fusion.x_ref
  83.5 27.1 %swap_exchange.1 = f32[32,32,128]{2,1,0:T(8,128)} custom-call(f32[776,128]{1,0:T(8,128)} %pad_maximum_fusion.x_ref), custom_call_target="tpu_custom_call" | custom-call | tf_op jit(solution)/shard_map/swap_exchange/pallas_call | solution.py:98
  110.6 1.7 reshape.35
  112.3 1.6 copy.22
  113.9 1.8 %reshape.36 = f32[64,8,256]{2,1,0:T(8,128)S(1)} reshape(f32[32,2,8,4,64]{4,3,2,1,0:T(4,128)} %copy.22) | data formatting | bytes 1048576 | tf_op jit(solution)/shard_map/reshape | solution.py:364
  115.8 5.1 %fusion.rebuilt_ref = f32[58,8,2048]{2,1,0:T(8,128)} fusion(f32[64,8,256]{2,1,0:T(8,128)S(1)} %reshape.36, f32[2048,256]{1,0:T(8,128)S(1)} %copy-done), kind=kOutput, calls=%fused_computation.1 | convolution fusion | flops 2919235584 | bytes 6422528 | tf_op jit(solution)/shard_map/xpb,yb->xpy/dot_general | solution.py:366
  120.9 34.1 %similarity_maps.1 = (f32[48,8,2048]{2,1,0:T(8,128)}, f32[48,8,2048]{2,1,0:T(8,128)}, f32[48,8,2048]{2,1,0:T(8,128)}, f32[2,8,128]{2,1,0:T(8,128)}) custom-call(f32[5,8,2048]{2,1,0:T(8,128)} %collective-permute-done.low_ref, f32[48,8,2048]{2,1,0:T(8,128)} %init_ref.1, f32[5,8,2048]{2,1,0:T(8,128)} %collective-permute-done.1.high_ref, ...), custom_call_target="tpu_custom_call" | custom-call | tf_op jit(solution)/shard_map/similarity_maps/pallas_call | solution.py:299
  155.0 14.7 %stats_exchange.1 = (f32[1,1]{1,0:T(1,128)}, f32[8,1]{1,0:T(8,128)}) custom-call(f32[2,8,128]{2,1,0:T(8,128)} %get-tuple-element.11.x_ref), custom_call_target="tpu_custom_call" | custom-call | tf_op jit(solution)/shard_map/stats_exchange/pallas_call | solution.py:133
  169.7 1.3 reduce
  (5 shorter events, 0.0 us)
Async XLA Ops:
  0.6 115.1 %copy-start = (f32[2048,256]{1,0:T(8,128)S(1)}, f32[2048,256]{1,0:T(8,128)}, u32[]{:S(2)}) copy-start(f32[2048,256]{1,0:T(8,128)} %param.8) | copy-start | bytes 6291460
  2.7 118.2 %collective-permute-start.1 = (f32[5,8,2048]{2,1,0:T(8,128)}, f32[5,8,2048]{2,1,0:T(8,128)}, u32[]{:S(2)}, u32[]{:S(2)}) collective-permute-start(f32[5,8,2048]{2,1,0:T(8,128)} %get-tuple-element.17), channel_id=1, source_target_pairs={{1,0},{2,1},{3,2},{4,3},{5,4},{6,5},{7,6},{8,7},{9,8},{10,9},{11,1... | collective-permute-start | bytes 983048 | tf_op jit(solution)/shard_map/ppermute | solution.py:330
  4.0 116.9 %collective-permute-start = (f32[5,8,2048]{2,1,0:T(8,128)S(1)}, f32[5,8,2048]{2,1,0:T(8,128)}, u32[]{:S(2)}, u32[]{:S(2)}) collective-permute-start(f32[5,8,2048]{2,1,0:T(8,128)S(1)} %get-tuple-element.18), channel_id=1, source_target_pairs={{0,1},{1,2},{2,3},{3,4},{4,5},{5,6},{6,7},{7,8},{8,9},{9,10},{10,1... | collective-permute-start | bytes 983048 | tf_op jit(solution)/shard_map/ppermute | solution.py:329

commit v3 on v2

--- a/solution.py
+++ b/solution.py
@@ -50,33 +50,98 @@
     return lambda: lax.fori_loop(1, count, wait, 0)
 
 
-def sum_kernel(count, x_ref, out_ref, received, send_sem, recv_sem):
+def halving_orders(count, units):
+    bits = [1 << j for j in range(count.bit_length() - 1)]
+    rest = bits[1:]
+    streams = max(1, min(3, units, len(rest)))
+    return [bits[:1] + rest[k:] + rest[:k] for k in range(streams)]
+
+
+def sum_kernel(count, orders, spans, x_ref, out_ref, *scratch):
+    streams = len(orders)
+    regions = scratch[:streams]
+    send_sem, recv_sem = scratch[streams:]
     me = lax.axis_index("rank")
-    greet(me, count)
-    finish = exchange(me, count, lambda peer: x_ref.at[peer], received, send_sem, recv_sem)
-    received[me] = x_ref[me]
-    finish()
-    out_ref[...] = received[0]
-
-    def add(index, carry):
-        out_ref[...] += received[index]
-        return carry
-
-    lax.fori_loop(1, count, add, 0)
+
+    def bit_of(bit):
+        return lax.rem(me // bit, 2)
+
+    def partner(bit):
+        return me + bit - 2 * bit * bit_of(bit)
+
+    barrier = pltpu.get_barrier_semaphore()
+    for bit in orders[0]:
+        pl.semaphore_signal(barrier, inc=1, device_id={"rank": partner(bit)})
+    pl.semaphore_wait(barrier, len(orders[0]))
+
+    def first_slot(stage):
+        return count - (count >> stage)
+
+    def held_at(stream, stage, index):
+        if stage:
+            return regions[stream].at[first_slot(stage - 1) + index]
+        place = sum(
+            lax.rem(index // (1 << j), 2) * bit for j, bit in enumerate(orders[stream])
+        )
+        start, size = spans[stream]
+        return x_ref.at[place, pl.ds(start, size)]
+
+    def copy_of(stream, stage, index):
+        bit = orders[stream][stage]
+        slot = first_slot(stage) + index
+        return pltpu.make_async_remote_copy(
+            src_ref=held_at(stream, stage, 1 - bit_of(bit) + 2 * index),
+            dst_ref=regions[stream].at[slot],
+            send_sem=send_sem.at[stream, slot],
+            recv_sem=recv_sem.at[stream, slot],
+            device_id={"rank": partner(bit)},
+        )
+
+    def begin(stream, stage):
+        def start(index, carry):
+            copy_of(stream, stage, index).start()
+            return carry
+
+        lax.fori_loop(0, count >> (stage + 1), start, 0)
+
+    def complete(stream, stage):
+        def add(index, carry):
+            copy_of(stream, stage, index).wait()
+            slot = first_slot(stage) + index
+            mine = held_at(stream, stage, bit_of(orders[stream][stage]) + 2 * index)
+            regions[stream][slot] += mine[...]
+            return carry
+
+        lax.fori_loop(0, count >> (stage + 1), add, 0)
+
+    stages = len(orders[0])
+    for stream in range(streams):
+        begin(stream, 0)
+    for stage in range(stages):
+        for stream in range(streams):
+            complete(stream, stage)
+            if stage + 1 < stages:
+                begin(stream, stage + 1)
+    for stream, (start, size) in enumerate(spans):
+        out_ref[pl.ds(start, size)] = regions[stream][count - 2]
 
 
 def sum_exchange(x):
-    count = x.shape[0]
+    count, rows, across = x.shape
+    units = rows // 8
+    orders = halving_orders(count, units)
+    share = [units // len(orders) + (k < units % len(orders)) for k in range(len(orders))]
+    spans = [(8 * sum(share[:k]), 8 * share[k]) for k in range(len(orders))]
     return pl.pallas_call(
-        functools.partial(sum_kernel, count),
+        functools.partial(sum_kernel, count, orders, spans),
         name="sum_exchange",
         out_shape=jax.ShapeDtypeStruct(x.shape[1:], x.dtype),
         in_specs=[pl.BlockSpec(memory_space=pltpu.VMEM)],
         out_specs=pl.BlockSpec(memory_space=pltpu.VMEM),
-        scratch_shapes=[
-            pltpu.VMEM(x.shape, x.dtype),
-            pltpu.SemaphoreType.DMA((count,)),
-            pltpu.SemaphoreType.DMA((count,)),
+        scratch_shapes=[pltpu.VMEM((count - 1, size, across), x.dtype) for _, size in spans]
+        + [
+            pltpu.SemaphoreType.DMA((len(orders), count - 1)),
+            pltpu.SemaphoreType.DMA((len(orders), count - 1)),
         ],
         compiler_params=pltpu.CompilerParams(collective_id=0, has_side_effects=True),
     )(x)
@@ -337,31 +402,24 @@
 
     pack = lanes // width
     extended = length + 2 * margin
-    before = -(-margin // pack) * pack
-    each = -(-(before - margin + extended) // (8 * pack)) * 8
-    if length % (8 * pack) == 0:
-        stride = length // pack
-        last = (count - 1) * length + each * pack - before - along
-        blocks = jnp.pad(x_factor, ((before, last), (0, 0)))
-    else:
+    each = -(-extended // (8 * pack)) * 8
+    expanded = jnp.einsum("xa,ba->xb", x_factor, owned, precision=exact)
+    total = (count - 1) * length + each
+    padded = jnp.pad(expanded, ((margin, pack * each), (0, 0)))
+    expanded = jnp.concatenate(
+        [padded[h * each:h * each + total] for h in range(pack)], axis=1
+    )
+    stride = length
+    if length % 8:
         stride = each
-        padded = jnp.pad(x_factor, ((before, each * pack), (0, 0)))
-        blocks = jnp.concatenate(
-            [padded[d * length:d * length + each * pack] for d in range(count)]
+        expanded = jnp.concatenate(
+            [expanded[d * length:d * length + each] for d in range(count)]
         )
-    blocks = blocks.reshape(-1, pack, rank)
-    expanded = jnp.concatenate(
-        [
-            jnp.einsum("xa,ba->xb", blocks[:, h], owned, precision=exact)
-            for h in range(pack)
-        ],
-        axis=1,
-    )
     arrived = swap_exchange(expanded, count, stride, each)
     rows = (
         arrived.reshape(planes, parts, each, pack, width)
-        .transpose(2, 3, 0, 1, 4)
-        .reshape(each * pack, planes, rank)[before - margin:before - margin + extended]
+        .transpose(3, 2, 0, 1, 4)
+        .reshape(each * pack, planes, rank)[:extended]
     )
     rebuilt = jnp.einsum("xpb,yb->xpy", rows, y_factor, precision=exact)
     five, seven, eleven, stats = similarity_maps(low, initial, high, rebuilt)

time: 173 us -> 131 us (0.76)
  Pallas kernels: 124 us -> 93.6 us
  local copies, waits for them, and re-layouts: 23.5 us -> 11.7 us
    pallas_call x1, Pallas kernels: 47.8 us -> 29.6 us  [sum_exchange(): pl.pallas_call(functools.partial(sum_kernel, count, orders, spans), name=...]
    pallas_call x1, Pallas kernels: 27.1 us -> 15.1 us  [swap_exchange(): pl.pallas_call(functools.partial(swap_kernel, count, stride, each), name=...]
    slice x1, local copies, waits for them, and re-layouts: 4.14 us -> 0.11 us  [body(): padded[h * each:h * each + total]]
    reshape x3 -> x2, local copies, waits for them, and re-layouts: 6.51 us -> 3.49 us  [the longest x1 1.83 us: body(): rows = arrived.reshape(planes, parts, each, pack, width).transpose(3, 2,...]
    pad x1 -> x0, local copies, waits for them, and re-layouts: 2.66 us -> none  [body(): blocks = jnp.pad(x_factor, ((before, last), (0, 0)))]
    dot_general x2 -> x1, matrix products: 3.53 us -> 2.82 us  [body(): expanded = jnp.einsum('xa,ba->xb', x_factor, owned, precision=exact)]
  transfers between devices with their start and end apart: 2 -> 2, of which waited for: 0 -> 0; matrix products, arithmetic and copies ran while one was open for 22% -> 20% of each run, Pallas kernels for 43% -> 34%
where the time goes in v3:
time: 131 us; the launch traced here: 130 us
  Pallas kernels  93.6 us (71%)
  matrix products  13.6 us (10%)
  local copies, waits for them, and re-layouts  11.7 us (9%)
  starting transfers between devices  5.06 us (4%)
  other arithmetic  3.78 us (3%)
  between operations  2.42 us (2%)
    pallas_call x1, Pallas kernels, similarity_maps(): pl.pallas_call(functools.partial(map_kernel, length, rows_step, lag), nam...  34.1 us
    pallas_call x1, Pallas kernels, sum_exchange(): pl.pallas_call(functools.partial(sum_kernel, count, orders, spans), name=...  29.6 us
    pallas_call x1, Pallas kernels, swap_exchange(): pl.pallas_call(functools.partial(swap_kernel, count, stride, each), name=...  15.1 us
    pallas_call x1, Pallas kernels, stats_exchange(): pl.pallas_call(functools.partial(stats_kernel, count, cells), name='stats...  14.9 us
    dot_general x1, matrix products, body(): partial = jnp.einsum('kab,kp->pba', core, picked, precision=exact)  5.75 us
    dot_general x1, matrix products, body(): rebuilt = jnp.einsum('xpb,yb->xpy', rows, y_factor, precision=exact)  5.08 us
    ppermute x1, starting transfers between devices, body(): low = lax.ppermute(initial[length - margin:], 'rank', forward)  3.78 us
    transpose x1, local copies, waits for them, and re-layouts, body(): partial = jnp.einsum('kab,kp->pba', core, picked, precision=exact)  2.89 us
  transfers between devices with their start and end apart: 2, of which 0 were waited for; matrix products, arithmetic and copies ran while one was open for 20% of the time, Pallas kernels for 34%

profile of v3, /device:TPU:0, one launch (start us, length us, event | category | flops | bytes accessed | tf_op | source)
XLA Modules:
  0.0 130.3 jit_solution(12959970019156867601)
XLA Ops:
  0.6 0.0 copy-start
  0.6 2.0 %fusion.12 = (f32[5,8,2048]{2,1,0:T(8,128)}, f32[5,8,2048]{2,1,0:T(8,128)S(1)}) fusion(f32[48,8,2048]{2,1,0:T(8,128)} %init_ref.1), kind=kLoop, calls=%fused_computation.18 | loop fusion | bytes 1310720 | tf_op jit(solution)/shard_map/slice | solution.py:395
  2.6 1.3 collective-permute-start.1
  3.9 3.8 %collective-permute-start = (f32[5,8,2048]{2,1,0:T(8,128)S(1)}, f32[5,8,2048]{2,1,0:T(8,128)}, u32[]{:S(2)}, u32[]{:S(2)}) collective-permute-start(f32[5,8,2048]{2,1,0:T(8,128)S(1)} %get-tuple-element.18), channel_id=1, source_target_pairs={{0,1},{1,2},{2,3},{3,4},{4,5},{5,6},{6,7},{7,8},{8,9},{9,10},{10,1... | collective-permute-start | bytes 983048 | tf_op jit(solution)/shard_map/ppermute | solution.py:394
  7.7 0.7 compare_and_fusion
  8.4 0.7 compare_select_fusion
  9.0 1.1 copy.16
  10.1 0.6 gather_fusion
  10.7 5.8 %fusion.4 = f32[8,256,256]{1,0,2:T(8,128)} fusion(f32[8,256,256]{2,1,0:T(8,128)} %param.6, f32[8,8]{1,0:T(8,128)S(1)} %gather_fusion, pred[8]{0:T(512)(128)(4,1)S(1)} %compare_and_fusion), kind=kOutput, calls=%fused_computation.6 | convolution fusion | flops 50331712 | bytes 4194568 | tf_op jit(solution)/shard_map/kab,kp->pba/dot_general | solution.py:400
  16.4 2.9 %copy.18 = f32[8,256,256]{2,1,0:T(8,128)} copy(f32[8,256,256]{1,0,2:T(8,128)} %fusion.4) | data formatting | bytes 4194304 | tf_op jit(solution)/shard_map/kab,kp->pba/transpose | solution.py:400
  19.3 29.6 %sum_exchange.1 = f32[64,256]{1,0:T(8,128)} custom-call(f32[32,64,256]{2,1,0:T(8,128)} %bitcast.16), custom_call_target="tpu_custom_call" | custom-call | tf_op jit(solution)/shard_map/sum_exchange/pallas_call | solution.py:135
  48.9 2.8 %convolution_bitcast_fusion = f32[1536,64]{1,0:T(8,128)S(1)} fusion(f32[64,256]{1,0:T(8,128)} %sum_exchange.1, f32[1536,256]{1,0:T(8,128)} %param.7), kind=kOutput, calls=%fused_computation.1 | convolution fusion | flops 301989888 | bytes 2031616 | tf_op jit(solution)/shard_map/xa,ba->xb/dot_general | solution.py:406
  51.7 0.1 pad_slice_fusion.1
  51.8 1.1 pad_maximum_fusion.x_ref
  53.0 15.1 %swap_exchange.1 = f32[32,32,128]{2,1,0:T(8,128)} custom-call(f32[1520,128]{1,0:T(8,128)} %pad_maximum_fusion.x_ref), custom_call_target="tpu_custom_call" | custom-call | tf_op jit(solution)/shard_map/swap_exchange/pallas_call | solution.py:163
  68.1 1.7 %reshape.31 = f32[8,4,32,2,64]{4,3,2,1,0:T(2,128)S(1)} reshape(f32[32,32,128]{2,1,0:T(8,128)} %swap_exchange.1) | data formatting | bytes 1048576 | tf_op jit(solution)/shard_map/reshape | solution.py:420
  69.8 1.6 %copy.20 = f32[2,32,8,4,64]{4,3,2,1,0:T(4,128)} copy(f32[2,32,8,4,64]{4,0,1,3,2:T(2,128)S(1)} %bitcast.17) | data formatting | bytes 1048576 | tf_op jit(solution)/shard_map/transpose | solution.py:421
  71.4 1.8 %reshape.32 = f32[64,8,256]{2,1,0:T(8,128)S(1)} reshape(f32[2,32,8,4,64]{4,3,2,1,0:T(4,128)} %copy.20) | data formatting | bytes 1048576 | tf_op jit(solution)/shard_map/reshape | solution.py:422
  73.3 5.1 %fusion.rebuilt_ref = f32[58,8,2048]{2,1,0:T(8,128)} fusion(f32[64,8,256]{2,1,0:T(8,128)S(1)} %reshape.32, f32[2048,256]{1,0:T(8,128)S(1)} %copy-done), kind=kOutput, calls=%fused_computation.2 | convolution fusion | flops 2919235584 | bytes 6422528 | tf_op jit(solution)/shard_map/xpb,yb->xpy/dot_general | solution.py:424
  78.3 0.0 collective-permute-done.1.high_ref
  78.3 0.0 collective-permute-done.low_ref
  78.3 34.1 %similarity_maps.1 = (f32[48,8,2048]{2,1,0:T(8,128)}, f32[48,8,2048]{2,1,0:T(8,128)}, f32[48,8,2048]{2,1,0:T(8,128)}, f32[2,8,128]{2,1,0:T(8,128)}) custom-call(f32[5,8,2048]{2,1,0:T(8,128)} %collective-permute-done.low_ref, f32[48,8,2048]{2,1,0:T(8,128)} %init_ref.1, f32[5,8,2048]{2,1,0:T(8,128)} %collective-permute-done.1.high_ref, ...), custom_call_target="tpu_custom_call" | custom-call | tf_op jit(solution)/shard_map/similarity_maps/pallas_call | solution.py:364
  112.4 14.9 %stats_exchange.1 = (f32[1,1]{1,0:T(1,128)}, f32[8,1]{1,0:T(8,128)}) custom-call(f32[2,8,128]{2,1,0:T(8,128)} %get-tuple-element.11.x_ref), custom_call_target="tpu_custom_call" | custom-call | tf_op jit(solution)/shard_map/stats_exchange/pallas_call | solution.py:198
  127.3 1.3 %reduce = f32[8]{0:T(128)} reduce(f32[8,1]{1,0:T(8,128)} %get-tuple-element.13, f32[]{:T(128)} %constant.24), dimensions={1}, to_apply=%get-tuple-element.13.reduce_sub_computation | reduce | bytes 68 | tf_op jit(solution)/shard_map/stats_exchange/pallas_call | solution.py:198
  (2 shorter events, 0.0 us)
Async XLA Ops:
  0.6 72.6 %copy-start = (f32[2048,256]{1,0:T(8,128)S(1)}, f32[2048,256]{1,0:T(8,128)}, u32[]{:S(2)}) copy-start(f32[2048,256]{1,0:T(8,128)} %param.8) | copy-start | bytes 6291460
  2.6 75.7 %collective-permute-start.1 = (f32[5,8,2048]{2,1,0:T(8,128)}, f32[5,8,2048]{2,1,0:T(8,128)}, u32[]{:S(2)}, u32[]{:S(2)}) collective-permute-start(f32[5,8,2048]{2,1,0:T(8,128)} %get-tuple-element.17), channel_id=1, source_target_pairs={{1,0},{2,1},{3,2},{4,3},{5,4},{6,5},{7,6},{8,7},{9,8},{10,9},{11,1... | collective-permute-start | bytes 983048 | tf_op jit(solution)/shard_map/ppermute | solution.py:395
  3.9 74.4 %collective-permute-start = (f32[5,8,2048]{2,1,0:T(8,128)S(1)}, f32[5,8,2048]{2,1,0:T(8,128)}, u32[]{:S(2)}, u32[]{:S(2)}) collective-permute-start(f32[5,8,2048]{2,1,0:T(8,128)S(1)} %get-tuple-element.18), channel_id=1, source_target_pairs={{0,1},{1,2},{2,3},{3,4},{4,5},{5,6},{6,7},{7,8},{8,9},{9,10},{10,1... | collective-permute-start | bytes 983048 | tf_op jit(solution)/shard_map/ppermute | solution.py:394

commit v4 on v3

--- a/solution.py
+++ b/solution.py
@@ -174,21 +174,29 @@
     )(x)
 
 
-def stats_kernel(count, cells, x_ref, error_ref, psnr_ref, received, send_sem, recv_sem):
+def stats_kernel(count, cells, x_ref, error_ref, psnr_ref, held, received, send_sem, recv_sem):
     me = lax.axis_index("rank")
-    greet(me, count)
-    finish = exchange(me, count, lambda peer: x_ref, received, send_sem, recv_sem)
-    received[me] = x_ref[...]
-    finish()
-    largest = received[0, 0]
-    total = received[0, 1]
-
-    def add(index, carry):
-        return jnp.maximum(carry[0], received[index, 0]), carry[1] + received[index, 1]
-
-    largest, total = lax.fori_loop(1, count, add, (largest, total))
-    error_ref[...] = jnp.max(largest, keepdims=True)
-    mean_square = jnp.sum(total, axis=1, keepdims=True) / cells
+    bits = [1 << j for j in range(count.bit_length() - 1)]
+    partners = [me + bit - 2 * bit * lax.rem(me // bit, 2) for bit in bits]
+    barrier = pltpu.get_barrier_semaphore()
+    for partner in partners:
+        pl.semaphore_signal(barrier, inc=1, device_id={"rank": partner})
+    pl.semaphore_wait(barrier, len(bits))
+    held[0] = x_ref[...]
+    for stage, partner in enumerate(partners):
+        copy = pltpu.make_async_remote_copy(
+            src_ref=held.at[stage],
+            dst_ref=received.at[stage],
+            send_sem=send_sem.at[stage],
+            recv_sem=recv_sem.at[stage],
+            device_id={"rank": partner},
+        )
+        copy.start()
+        copy.wait()
+        held[stage + 1, 0] = jnp.maximum(held[stage, 0], received[stage, 0])
+        held[stage + 1, 1] = held[stage, 1] + received[stage, 1]
+    error_ref[...] = jnp.max(held[len(bits), 0], keepdims=True)
+    mean_square = jnp.sum(held[len(bits), 1], axis=1, keepdims=True) / cells
     psnr = 10.0 * (jnp.log(peak_value * peak_value / (mean_square + epsilon)) / jnp.log(10.0))
     psnr_ref[...] = psnr
 
@@ -205,9 +213,10 @@
         in_specs=[pl.BlockSpec(memory_space=pltpu.VMEM)],
         out_specs=(pl.BlockSpec(memory_space=pltpu.VMEM),) * 2,
         scratch_shapes=[
-            pltpu.VMEM((count,) + x.shape, x.dtype),
-            pltpu.SemaphoreType.DMA((count,)),
-            pltpu.SemaphoreType.DMA((count,)),
+            pltpu.VMEM((count.bit_length(),) + x.shape, x.dtype),
+            pltpu.VMEM((count.bit_length(),) + x.shape, x.dtype),
+            pltpu.SemaphoreType.DMA((count.bit_length(),)),
+            pltpu.SemaphoreType.DMA((count.bit_length(),)),
         ],
         compiler_params=pltpu.CompilerParams(collective_id=2, has_side_effects=True),
     )(x)

time: 131 us -> 135 us (1.031)
  Pallas kernels: 93.6 us -> 97.9 us
    pallas_call x1, Pallas kernels: 14.9 us -> 19.1 us  [stats_exchange(): pl.pallas_call(functools.partial(stats_kernel, count, cells), name='stats...]
  transfers between devices with their start and end apart: 2 -> 2, of which waited for: 0 -> 0; matrix products, arithmetic and copies ran while one was open for 20% -> 19% of each run, Pallas kernels for 34% -> 33%
where the time goes in v4:
time: 135 us
  Pallas kernels  97.9 us (73%)
  matrix products  13.6 us (10%)
  local copies, waits for them, and re-layouts  11.7 us (9%)
  starting transfers between devices  5.06 us (4%)
  other arithmetic  3.78 us (3%)
  between operations  2.42 us (2%)
    pallas_call x1, Pallas kernels, similarity_maps(): pl.pallas_call(functools.partial(map_kernel, length, rows_step, lag), nam...  34.1 us
    pallas_call x1, Pallas kernels, sum_exchange(): pl.pallas_call(functools.partial(sum_kernel, count, orders, spans), name=...  29.6 us
    pallas_call x1, Pallas kernels, stats_exchange(): pl.pallas_call(functools.partial(stats_kernel, count, cells), name='stats...  19.1 us
    pallas_call x1, Pallas kernels, swap_exchange(): pl.pallas_call(functools.partial(swap_kernel, count, stride, each), name=...  15.1 us
    dot_general x1, matrix products, body(): partial = jnp.einsum('kab,kp->pba', core, picked, precision=exact)  5.75 us
    dot_general x1, matrix products, body(): rebuilt = jnp.einsum('xpb,yb->xpy', rows, y_factor, precision=exact)  5.08 us
    ppermute x1, starting transfers between devices, body(): low = lax.ppermute(initial[length - margin:], 'rank', forward)  3.78 us
    transpose x1, local copies, waits for them, and re-layouts, body(): partial = jnp.einsum('kab,kp->pba', core, picked, precision=exact)  2.89 us
  transfers between devices with their start and end apart: 2, of which 0 were waited for; matrix products, arithmetic and copies ran while one was open for 19% of the time, Pallas kernels for 33%

profile of v4, /device:TPU:0, one launch (start us, length us, event | category | flops | bytes accessed | tf_op | source)
XLA Modules:
  0.0 134.6 jit_solution(15557936391509535239)
XLA Ops:
  0.6 0.0 copy-start
  0.6 2.0 %fusion.12 = (f32[5,8,2048]{2,1,0:T(8,128)}, f32[5,8,2048]{2,1,0:T(8,128)S(1)}) fusion(f32[48,8,2048]{2,1,0:T(8,128)} %init_ref.1), kind=kLoop, calls=%fused_computation.18 | loop fusion | bytes 1310720 | tf_op jit(solution)/shard_map/slice | solution.py:404
  2.6 1.3 collective-permute-start.1
  3.9 3.8 %collective-permute-start = (f32[5,8,2048]{2,1,0:T(8,128)S(1)}, f32[5,8,2048]{2,1,0:T(8,128)}, u32[]{:S(2)}, u32[]{:S(2)}) collective-permute-start(f32[5,8,2048]{2,1,0:T(8,128)S(1)} %get-tuple-element.18), channel_id=1, source_target_pairs={{0,1},{1,2},{2,3},{3,4},{4,5},{5,6},{6,7},{7,8},{8,9},{9,10},{10,1... | collective-permute-start | bytes 983048 | tf_op jit(solution)/shard_map/ppermute | solution.py:403
  7.7 0.7 compare_and_fusion
  8.4 0.7 compare_select_fusion
  9.0 1.1 copy.16
  10.1 0.6 gather_fusion
  10.7 5.8 %fusion.4 = f32[8,256,256]{1,0,2:T(8,128)} fusion(f32[8,256,256]{2,1,0:T(8,128)} %param.6, f32[8,8]{1,0:T(8,128)S(1)} %gather_fusion, pred[8]{0:T(512)(128)(4,1)S(1)} %compare_and_fusion), kind=kOutput, calls=%fused_computation.6 | convolution fusion | flops 50331712 | bytes 4194568 | tf_op jit(solution)/shard_map/kab,kp->pba/dot_general | solution.py:409
  16.4 2.9 %copy.18 = f32[8,256,256]{2,1,0:T(8,128)} copy(f32[8,256,256]{1,0,2:T(8,128)} %fusion.4) | data formatting | bytes 4194304 | tf_op jit(solution)/shard_map/kab,kp->pba/transpose | solution.py:409
  19.3 29.6 %sum_exchange.1 = f32[64,256]{1,0:T(8,128)} custom-call(f32[32,64,256]{2,1,0:T(8,128)} %bitcast.16), custom_call_target="tpu_custom_call" | custom-call | tf_op jit(solution)/shard_map/sum_exchange/pallas_call | solution.py:135
  48.9 2.8 %convolution_bitcast_fusion = f32[1536,64]{1,0:T(8,128)S(1)} fusion(f32[64,256]{1,0:T(8,128)} %sum_exchange.1, f32[1536,256]{1,0:T(8,128)} %param.7), kind=kOutput, calls=%fused_computation.1 | convolution fusion | flops 301989888 | bytes 2031616 | tf_op jit(solution)/shard_map/xa,ba->xb/dot_general | solution.py:415
  51.7 0.1 pad_slice_fusion.1
  51.8 1.1 pad_maximum_fusion.x_ref
  53.0 15.1 %swap_exchange.1 = f32[32,32,128]{2,1,0:T(8,128)} custom-call(f32[1520,128]{1,0:T(8,128)} %pad_maximum_fusion.x_ref), custom_call_target="tpu_custom_call" | custom-call | tf_op jit(solution)/shard_map/swap_exchange/pallas_call | solution.py:163
  68.1 1.7 %reshape.31 = f32[8,4,32,2,64]{4,3,2,1,0:T(2,128)S(1)} reshape(f32[32,32,128]{2,1,0:T(8,128)} %swap_exchange.1) | data formatting | bytes 1048576 | tf_op jit(solution)/shard_map/reshape | solution.py:429
  69.8 1.6 %copy.20 = f32[2,32,8,4,64]{4,3,2,1,0:T(4,128)} copy(f32[2,32,8,4,64]{4,0,1,3,2:T(2,128)S(1)} %bitcast.17) | data formatting | bytes 1048576 | tf_op jit(solution)/shard_map/transpose | solution.py:430
  71.4 1.8 %reshape.32 = f32[64,8,256]{2,1,0:T(8,128)S(1)} reshape(f32[2,32,8,4,64]{4,3,2,1,0:T(4,128)} %copy.20) | data formatting | bytes 1048576 | tf_op jit(solution)/shard_map/reshape | solution.py:431
  73.3 5.1 %fusion.rebuilt_ref = f32[58,8,2048]{2,1,0:T(8,128)} fusion(f32[64,8,256]{2,1,0:T(8,128)S(1)} %reshape.32, f32[2048,256]{1,0:T(8,128)S(1)} %copy-done), kind=kOutput, calls=%fused_computation.2 | convolution fusion | flops 2919235584 | bytes 6422528 | tf_op jit(solution)/shard_map/xpb,yb->xpy/dot_general | solution.py:433
  78.3 0.0 collective-permute-done.1.high_ref
  78.3 0.0 collective-permute-done.low_ref
  78.3 34.1 %similarity_maps.1 = (f32[48,8,2048]{2,1,0:T(8,128)}, f32[48,8,2048]{2,1,0:T(8,128)}, f32[48,8,2048]{2,1,0:T(8,128)}, f32[2,8,128]{2,1,0:T(8,128)}) custom-call(f32[5,8,2048]{2,1,0:T(8,128)} %collective-permute-done.low_ref, f32[48,8,2048]{2,1,0:T(8,128)} %init_ref.1, f32[5,8,2048]{2,1,0:T(8,128)} %collective-permute-done.1.high_ref, ...), custom_call_target="tpu_custom_call" | custom-call | tf_op jit(solution)/shard_map/similarity_maps/pallas_call | solution.py:373
  112.4 19.1 %stats_exchange.1 = (f32[1,1]{1,0:T(1,128)}, f32[8,1]{1,0:T(8,128)}) custom-call(f32[2,8,128]{2,1,0:T(8,128)} %get-tuple-element.11.x_ref), custom_call_target="tpu_custom_call" | custom-call | tf_op jit(solution)/shard_map/stats_exchange/pallas_call | solution.py:206
  131.6 1.3 reduce
  (2 shorter events, 0.0 us)
Async XLA Ops:
  0.6 72.6 %copy-start = (f32[2048,256]{1,0:T(8,128)S(1)}, f32[2048,256]{1,0:T(8,128)}, u32[]{:S(2)}) copy-start(f32[2048,256]{1,0:T(8,128)} %param.8) | copy-start | bytes 6291460
  2.6 75.7 %collective-permute-start.1 = (f32[5,8,2048]{2,1,0:T(8,128)}, f32[5,8,2048]{2,1,0:T(8,128)}, u32[]{:S(2)}, u32[]{:S(2)}) collective-permute-start(f32[5,8,2048]{2,1,0:T(8,128)} %get-tuple-element.17), channel_id=1, source_target_pairs={{1,0},{2,1},{3,2},{4,3},{5,4},{6,5},{7,6},{8,7},{9,8},{10,9},{11,1... | collective-permute-start | bytes 983048 | tf_op jit(solution)/shard_map/ppermute | solution.py:404
  3.9 74.4 %collective-permute-start = (f32[5,8,2048]{2,1,0:T(8,128)S(1)}, f32[5,8,2048]{2,1,0:T(8,128)}, u32[]{:S(2)}, u32[]{:S(2)}) collective-permute-start(f32[5,8,2048]{2,1,0:T(8,128)S(1)} %get-tuple-element.18), channel_id=1, source_target_pairs={{0,1},{1,2},{2,3},{3,4},{4,5},{5,6},{6,7},{7,8},{8,9},{9,10},{10,1... | collective-permute-start | bytes 983048 | tf_op jit(solution)/shard_map/ppermute | solution.py:403
